TPU v7x, 512 devices: a whole 4x8x8 slice. The times are simulated.
512 devices in a mesh: box: 32 (over y, z_hi, core), grp: 16 (over z_lo, x).
Axes of the slice: x: 4, y: 8, z: 8 (z_hi: 2, z_lo: 4; z = z_hi * 4 + z_lo), core: 2. Of those that a mesh axis runs over, the one named last changes fastest.
Arguments:
- impedance: bfloat16 [2, 32, 1, 2048, 2048], P(None, 'box', None, None, 'grp'), may hold values from -3 to 3
- face_order: int32 [32, 1, 16], replicated, may hold values from 0 to 15, each once within a row
Outputs:
- merged: bfloat16 [2, 32, 1, 4096, 2048], P(None, 'box', None, None, 'grp')
Inputs may be any that keep to these rules, and one draw needn't show every extreme that they name: `face_order`: each row lists the 16 face blocks of one box once; its first 3 entries are the blocks on the face shared with the sibling, the k-th facing the sibling's k-th.
All inputs are finite; a program needn't handle non-finite values.
Results may differ from a plain program's by a relative error of at most 0.0035.
Values may be sent and summed in bfloat16 or wider, within the bound.
No kernel may reach another device: no remote copies, remote signals or barrier semaphores. Data moves between devices by JAX's collectives and lax.ppermute only.
A program may use at most 64 MiB of HBM per device.

v0:
```python
import functools

import jax
import jax.numpy as jnp
from jax import lax
from jax.experimental import pallas as pl
from jax.experimental.pallas import tpu as pltpu
from jax.sharding import PartitionSpec as P


BLK = 128
MB = 3
IFACE = MB * BLK

PLACES = (
    (0, pl.ds(0, 2), pl.ds(0, 2), 0),
    (0, pl.ds(2, 3), 0, pl.ds(1, 3)),
    (0, pl.ds(5, 2), pl.ds(2, 2), 0),
    (1, pl.ds(0, 3), 1, pl.ds(1, 3)),
    (2, pl.ds(0, 2), pl.ds(2, 2), 1),
    (3, pl.ds(0, 2), pl.ds(2, 2), 3),
    (4, pl.ds(0, 2), pl.ds(2, 2), 2),
)


def exchange(block, axis, mask):
    count = lax.axis_size(axis)
    return lax.ppermute(block, axis, [(i, i ^ mask) for i in range(count)])


def stacked(pair, width):
    turned = jnp.concatenate([-pair[:, width:], pair[:, :width]], axis=1)
    return jnp.concatenate([pair, turned], axis=0)


def dot(a, b):
    return jnp.dot(a, b, preferred_element_type=jnp.float32)


def merge_kernel(
    order, own_in, *refs, points, width
):
    sides, (out, own, zc, out_v, in_sems, out_sems) = (refs[:5], refs[5:10]), refs[10:]
    piece = zc.shape[3]
    me = lax.axis_index("grp")
    box = lax.axis_index("box")
    x, z = lax.rem(me, 4), lax.div(me, 4)
    z_low, z_high = lax.rem(z, 2), lax.div(z, 2)
    parity = lax.rem(box, 2)
    twin = box + 1 - 2 * parity
    copies = [pltpu.make_async_copy(own_in, own, in_sems.at[0])]
    for side, arrays in enumerate(sides):
        for i, rows, zs, xs in PLACES:
            sem = in_sems.at[len(copies)]
            copies.append(pltpu.make_async_copy(arrays[i].at[rows], zc.at[side, zs, xs], sem))
    for c in copies:
        c.start()
    for c in copies:
        c.wait()

    def face_rows(side, holder, p):
        rows = []
        for j in range(MB):
            face = order[holder, j]
            src = p * 8 + lax.div(face, 2)
            zr = jnp.bitwise_xor(lax.div(src, 4), z)
            xr = jnp.bitwise_xor(lax.rem(src, 4), x)
            at = pl.multiple_of(lax.rem(face, 2) * BLK, BLK)
            rows.append(zc[side, zr, xr, pl.ds(at, BLK), :])
        return jnp.concatenate(rows, axis=0)

    zb = jnp.concatenate([face_rows(0, box, 0), face_rows(0, box, 1)], axis=1)
    zs = jnp.concatenate([face_rows(1, twin, 0), face_rows(1, twin, 1)], axis=1)
    first = lax.div(me * width, BLK)
    ext = jnp.float32(1.0)
    parts = []
    for j in range(MB):
        ext = jnp.where(order[box, j] == first, jnp.float32(0.0), ext)
    for p in range(2):
        rows = [
            own[p, pl.ds(pl.multiple_of(order[box, j] * BLK, BLK), BLK), :] for j in range(MB)
        ]
        parts.append(jnp.concatenate(rows, axis=0))
    start = jnp.concatenate(parts, axis=1).astype(jnp.float32) * ext

    def times(left, v, exact=False):
        high = v.astype(jnp.bfloat16)
        res = dot(left, stacked(high, width))
        if exact:
            return res
        low = (v - high.astype(jnp.float32)).astype(jnp.bfloat16)
        return res + dot(left, stacked(low, width))

    v = start
    for step in range(3):
        v = start + (1.0 / points) * times(zb, times(zs, v, exact=step == 0))
    resp = stacked(v.astype(jnp.bfloat16), width)
    echo = stacked(times(zs, v).astype(jnp.bfloat16), width)

    sent = []
    for xk in range(4):
        for zl in range(2):
            m = jnp.bitwise_xor(x, xk) + 4 * jnp.bitwise_xor(z_low, zl)
            rows = pl.ds(pl.multiple_of(m * piece, piece), piece)
            for side, right in ((0, echo), (1, resp)):
                zr = zc[side, zl + 2 * z_high, xk]
                zi = zc[side, zl + 2 - 2 * z_high, xk]
                acc = dot(jnp.concatenate([zr, zi], axis=1), right)
                half = jnp.bitwise_xor(parity, side)
                for p in range(2):
                    val = acc[:, p * width : (p + 1) * width]
                    if side == 0:
                        val = own[p, rows, :].astype(jnp.float32) * ext + val * (1.0 / points)
                    else:
                        val = val * -(points ** -0.5)
                    out_v[p, half, rows, :] = val.astype(jnp.bfloat16)
                view = (slice(None), half, rows)
                c = pltpu.make_async_copy(
                    out_v.at[view], out.at[view], out_sems.at[len(sent)]
                )
                c.start()
                sent.append(c)
    for c in sent:
        c.wait()


def shards(impedance, face_order):
    own_cols = impedance[:, 0, 0]
    points, width = own_cols.shape[1:]
    piece = 2 * points // 16
    box_here = lax.axis_index("box")
    own_order = lax.dynamic_index_in_dim(face_order, box_here, 0, keepdims=False)[0]
    spread = lax.all_to_all(own_cols.reshape(16, piece, width), "grp", 0, 0, tiled=True)
    mine = jnp.concatenate(
        [
            lax.dynamic_index_in_dim(spread, own_order[j] * BLK // width, 0, keepdims=False)
            for j in range(MB)
        ],
        axis=-1,
    )
    orders = face_order[:, 0]
    mine, orders = lax.optimization_barrier((mine, orders))
    z1, x1, x3, z3, x2, z2 = (
        exchange(mine, "grp", m)
        for m in (4, 1, 3, 12, 2, 8)
    )
    near = jnp.stack([x1, x2, x3])
    far = jnp.stack([z2, z3])
    every = jnp.stack([mine, z1, x1, x2, x3, z2, z3])
    late = [exchange(near, "grp", 4)]
    late += [exchange(far, "grp", k) for k in (1, 3, 2)]
    gathered = [every] + late
    gathered += [exchange(g, "box", 1) for g in gathered]
    anywhere = pl.BlockSpec(memory_space=pl.ANY)
    out = pl.pallas_call(
        functools.partial(merge_kernel, points=points, width=width),
        out_shape=jax.ShapeDtypeStruct((2, 2, points, width), jnp.bfloat16),
        in_specs=[pl.BlockSpec(memory_space=pltpu.SMEM)] + [anywhere] * 11,
        out_specs=anywhere,
        scratch_shapes=[
            pltpu.VMEM((2, points, width), jnp.bfloat16),
            pltpu.VMEM((2, 4, 4, piece, IFACE), jnp.bfloat16),
            pltpu.VMEM((2, 2, points, width), jnp.bfloat16),
            pltpu.SemaphoreType.DMA((17,)),
            pltpu.SemaphoreType.DMA((16,)),
        ],
        compiler_params=pltpu.CompilerParams(vmem_limit_bytes=24 << 20),
        name="merge",
    )(orders, own_cols, *gathered)
    return out.reshape(2, 1, 1, 2 * points, width)


def solution(mesh):
    in_specs = (P(None, "box", None, None, "grp"), P())
    out_specs = P(None, "box", None, None, "grp")
    return jax.shard_map(shards, mesh=mesh, in_specs=in_specs, out_specs=out_specs, check_vma=False)
```

profile of v0, /device:TPU:1, one launch (start us, length us, event | category | flops | bytes accessed | tf_op | source)
XLA Modules:
  0.0 112.0 jit_solution(17110340871361567718)
XLA Ops:
  0.0 10.5 %all-to-all-start = ((bf16[16,256,128]{2,1,0:T(8,128)(2,1)}), bf16[16,256,128]{2,1,0:T(8,128)(2,1)S(1)}, u32[]{:S(2)}, u32[]{:S(2)}) async-start(bf16[16,256,128]{2,1,0:T(8,128)(2,1)} %bitcast.29), calls=%async_computation | async-start | bytes 2097152 | tf_op jit(solution)/shard_map/all_to_all | solution.py:133
  10.5 0.6 constant_dynamic-slice_fusion.1
  13.1 0.1 copy.3
  13.1 19.7 %all-to-all-done = bf16[16,256,128]{2,1,0:T(8,128)(2,1)S(1)} async-done(((bf16[16,256,128]{2,1,0:T(8,128)(2,1)}), bf16[16,256,128]{2,1,0:T(8,128)(2,1)S(1)}, u32[]{:S(2)}, u32[]{:S(2)}) %all-to-all-start) | async-done | bytes 1048608 | tf_op jit(solution)/shard_map/all_to_all | solution.py:133
  32.9 5.1 %collective-permute-start.5 = (bf16[256,384]{1,0:T(8,128)(2,1)S(1)}, bf16[256,384]{1,0:T(8,128)(2,1)S(1)}, u32[]{:S(2)}, u32[]{:S(2)}) collective-permute-start(bf16[256,384]{1,0:T(8,128)(2,1)S(1)} %pad_maximum_fusion.2), channel_id=1, source_target_pairs={{0,12},{1,13},{2,14},{3,15},{4,8},{5,9},{6,10},{7,11},{8,4},{9,5},... | collective-permute-start | bytes 589832 | tf_op jit(solution)/shard_map/ppermute | solution.py:28
  38.1 4.1 %collective-permute-start.4 = (bf16[256,384]{1,0:T(8,128)(2,1)S(1)}, bf16[256,384]{1,0:T(8,128)(2,1)S(1)}, u32[]{:S(2)}, u32[]{:S(2)}) collective-permute-start(bf16[256,384]{1,0:T(8,128)(2,1)S(1)} %pad_maximum_fusion.2), channel_id=1, source_target_pairs={{0,8},{1,9},{2,10},{3,11},{4,12},{5,13},{6,14},{7,15},{8,0},{9,1},... | collective-permute-start | bytes 589832 | tf_op jit(solution)/shard_map/ppermute | solution.py:28
  42.2 3.2 %collective-permute-start.3 = (bf16[256,384]{1,0:T(8,128)(2,1)S(1)}, bf16[256,384]{1,0:T(8,128)(2,1)S(1)}, u32[]{:S(2)}, u32[]{:S(2)}) collective-permute-start(bf16[256,384]{1,0:T(8,128)(2,1)S(1)} %pad_maximum_fusion.2), channel_id=1, source_target_pairs={{0,3},{1,2},{2,1},{3,0},{4,7},{5,6},{6,5},{7,4},{8,11},{9,10},{10,... | collective-permute-start | bytes 589832 | tf_op jit(solution)/shard_map/ppermute | solution.py:28
  45.4 2.8 %collective-permute-start.2 = (bf16[256,384]{1,0:T(8,128)(2,1)S(1)}, bf16[256,384]{1,0:T(8,128)(2,1)S(1)}, u32[]{:S(2)}, u32[]{:S(2)}) collective-permute-start(bf16[256,384]{1,0:T(8,128)(2,1)S(1)} %pad_maximum_fusion.2), channel_id=1, source_target_pairs={{0,2},{1,3},{2,0},{3,1},{4,6},{5,7},{6,4},{7,5},{8,10},{9,11},{10,... | collective-permute-start | bytes 589832 | tf_op jit(solution)/shard_map/ppermute | solution.py:28
  48.2 2.0 %collective-permute-start = (bf16[256,384]{1,0:T(8,128)(2,1)S(1)}, bf16[256,384]{1,0:T(8,128)(2,1)S(1)}, u32[]{:S(2)}, u32[]{:S(2)}) collective-permute-start(bf16[256,384]{1,0:T(8,128)(2,1)S(1)} %pad_maximum_fusion.2), channel_id=1, source_target_pairs={{0,4},{1,5},{2,6},{3,7},{4,0},{5,1},{6,2},{7,3},{8,12},{9,13},{10,... | collective-permute-start | bytes 589832 | tf_op jit(solution)/shard_map/ppermute | solution.py:28
  50.3 9.3 %collective-permute-done = bf16[256,384]{1,0:T(8,128)(2,1)S(1)} collective-permute-done((bf16[256,384]{1,0:T(8,128)(2,1)S(1)}, bf16[256,384]{1,0:T(8,128)(2,1)S(1)}, u32[]{:S(2)}, u32[]{:S(2)}) %collective-permute-start) | collective-permute-done | bytes 196640 | tf_op jit(solution)/shard_map/ppermute | solution.py:28
  59.6 2.4 %collective-permute-start.1 = (bf16[256,384]{1,0:T(8,128)(2,1)S(1)}, bf16[256,384]{1,0:T(8,128)(2,1)S(1)}, u32[]{:S(2)}, u32[]{:S(2)}) collective-permute-start(bf16[256,384]{1,0:T(8,128)(2,1)S(1)} %pad_maximum_fusion.2), channel_id=1, source_target_pairs={{0,1},{1,0},{2,3},{3,2},{4,5},{5,4},{6,7},{7,6},{8,9},{9,8},{10,11... | collective-permute-start | bytes 589832 | tf_op jit(solution)/shard_map/ppermute | solution.py:28
  62.0 5.1 %collective-permute-done.1 = bf16[256,384]{1,0:T(8,128)(2,1)S(1)} collective-permute-done((bf16[256,384]{1,0:T(8,128)(2,1)S(1)}, bf16[256,384]{1,0:T(8,128)(2,1)S(1)}, u32[]{:S(2)}, u32[]{:S(2)}) %collective-permute-start.1) | collective-permute-done | bytes 196640 | tf_op jit(solution)/shard_map/ppermute | solution.py:28
  67.1 0.0 collective-permute-done.2
  67.2 0.0 collective-permute-done.3
  67.2 0.0 copy-start
  67.2 0.0 collective-permute-done.4
  67.3 0.0 collective-permute-done.5
  67.3 3.8 %collective-permute-start.10 = (bf16[7,256,384]{2,1,0:T(8,128)(2,1)S(1)}, bf16[7,256,384]{2,1,0:T(8,128)(2,1)S(1)}, u32[]{:S(2)}, u32[]{:S(2)}) collective-permute-start(bf16[7,256,384]{2,1,0:T(8,128)(2,1)S(1)} %constant_dynamic-update-slice_fusion.refs_0_), channel_id=1, source_target_pairs={{0,16},{16,0},{32,48},{48,32},{64,80},{80,64},{96,112},{112,96},{1... | collective-permute-start | bytes 4128776 | tf_op jit(solution)/shard_map/ppermute | solution.py:28
  71.1 0.1 pad_maximum_fusion
  71.2 1.9 %collective-permute-start.6 = (bf16[3,256,384]{2,1,0:T(8,128)(2,1)S(1)}, bf16[3,256,384]{2,1,0:T(8,128)(2,1)S(1)}, u32[]{:S(2)}, u32[]{:S(2)}) collective-permute-start(bf16[3,256,384]{2,1,0:T(8,128)(2,1)S(1)} %pad_maximum_fusion), channel_id=1, source_target_pairs={{0,4},{1,5},{2,6},{3,7},{4,0},{5,1},{6,2},{7,3},{8,12},{9,13},{10,... | collective-permute-start | bytes 1769480 | tf_op jit(solution)/shard_map/ppermute | solution.py:28
  73.2 4.8 %collective-permute-start.9 = (bf16[2,256,384]{2,1,0:T(8,128)(2,1)S(1)}, bf16[2,256,384]{2,1,0:T(8,128)(2,1)S(1)}, u32[]{:S(2)}, u32[]{:S(2)}) collective-permute-start(bf16[2,256,384]{2,1,0:T(8,128)(2,1)S(1)} %pad_maximum_fusion.1), channel_id=1, source_target_pairs={{0,2},{1,3},{2,0},{3,1},{4,6},{5,7},{6,4},{7,5},{8,10},{9,11},{10,... | collective-permute-start | bytes 1179656 | tf_op jit(solution)/shard_map/ppermute | solution.py:28
  78.0 1.9 %collective-permute-start.8 = (bf16[2,256,384]{2,1,0:T(8,128)(2,1)S(1)}, bf16[2,256,384]{2,1,0:T(8,128)(2,1)S(1)}, u32[]{:S(2)}, u32[]{:S(2)}) collective-permute-start(bf16[2,256,384]{2,1,0:T(8,128)(2,1)S(1)} %pad_maximum_fusion.1), channel_id=1, source_target_pairs={{0,3},{1,2},{2,1},{3,0},{4,7},{5,6},{6,5},{7,4},{8,11},{9,10},{10,... | collective-permute-start | bytes 1179656 | tf_op jit(solution)/shard_map/ppermute | solution.py:28
  79.9 2.2 %collective-permute-start.7 = (bf16[2,256,384]{2,1,0:T(8,128)(2,1)S(1)}, bf16[2,256,384]{2,1,0:T(8,128)(2,1)S(1)}, u32[]{:S(2)}, u32[]{:S(2)}) collective-permute-start(bf16[2,256,384]{2,1,0:T(8,128)(2,1)S(1)} %pad_maximum_fusion.1), channel_id=1, source_target_pairs={{0,1},{1,0},{2,3},{3,2},{4,5},{5,4},{6,7},{7,6},{8,9},{9,8},{10,11... | collective-permute-start | bytes 1179656 | tf_op jit(solution)/shard_map/ppermute | solution.py:28
  82.1 5.9 %collective-permute-done.6.refs_1_ = bf16[3,256,384]{2,1,0:T(8,128)(2,1)S(1)} collective-permute-done((bf16[3,256,384]{2,1,0:T(8,128)(2,1)S(1)}, bf16[3,256,384]{2,1,0:T(8,128)(2,1)S(1)}, u32[]{:S(2)}, u32[]{:S(2)}) %collective-permute-start.6) | collective-permute-done | bytes 589856 | tf_op jit(solution)/shard_map/ppermute | solution.py:28
  88.0 2.8 %collective-permute-start.11 = (bf16[3,256,384]{2,1,0:T(8,128)(2,1)S(1)}, bf16[3,256,384]{2,1,0:T(8,128)(2,1)S(1)}, u32[]{:S(2)}, u32[]{:S(2)}) collective-permute-start(bf16[3,256,384]{2,1,0:T(8,128)(2,1)S(1)} %collective-permute-done.6.refs_1_), channel_id=1, source_target_pairs={{0,16},{16,0},{32,48},{48,32},{64,80},{80,64},{96,112},{112,96},{1... | collective-permute-start | bytes 1769480 | tf_op jit(solution)/shard_map/ppermute | solution.py:28
  90.7 1.9 %collective-permute-start.14 = (bf16[2,256,384]{2,1,0:T(8,128)(2,1)S(1)}, bf16[2,256,384]{2,1,0:T(8,128)(2,1)S(1)}, u32[]{:S(2)}, u32[]{:S(2)}) collective-permute-start(bf16[2,256,384]{2,1,0:T(8,128)(2,1)S(1)} %collective-permute-done.9.refs_4_), channel_id=1, source_target_pairs={{0,16},{16,0},{32,48},{48,32},{64,80},{80,64},{96,112},{112,96},{1... | collective-permute-start | bytes 1179656 | tf_op jit(solution)/shard_map/ppermute | solution.py:28
  92.7 3.4 %collective-permute-done.8.refs_3_ = bf16[2,256,384]{2,1,0:T(8,128)(2,1)S(1)} collective-permute-done((bf16[2,256,384]{2,1,0:T(8,128)(2,1)S(1)}, bf16[2,256,384]{2,1,0:T(8,128)(2,1)S(1)}, u32[]{:S(2)}, u32[]{:S(2)}) %collective-permute-start.8) | collective-permute-done | bytes 393248 | tf_op jit(solution)/shard_map/ppermute | solution.py:28
  96.1 2.4 %collective-permute-start.13 = (bf16[2,256,384]{2,1,0:T(8,128)(2,1)S(1)}, bf16[2,256,384]{2,1,0:T(8,128)(2,1)S(1)}, u32[]{:S(2)}, u32[]{:S(2)}) collective-permute-start(bf16[2,256,384]{2,1,0:T(8,128)(2,1)S(1)} %collective-permute-done.8.refs_3_), channel_id=1, source_target_pairs={{0,16},{16,0},{32,48},{48,32},{64,80},{80,64},{96,112},{112,96},{1... | collective-permute-start | bytes 1179656 | tf_op jit(solution)/shard_map/ppermute | solution.py:28
  98.4 0.0 collective-permute-done.7.refs_2_
  98.4 2.0 %collective-permute-start.12 = (bf16[2,256,384]{2,1,0:T(8,128)(2,1)S(1)}, bf16[2,256,384]{2,1,0:T(8,128)(2,1)S(1)}, u32[]{:S(2)}, u32[]{:S(2)}) collective-permute-start(bf16[2,256,384]{2,1,0:T(8,128)(2,1)S(1)} %collective-permute-done.7.refs_2_), channel_id=1, source_target_pairs={{0,16},{16,0},{32,48},{48,32},{64,80},{80,64},{96,112},{112,96},{1... | collective-permute-start | bytes 1179656 | tf_op jit(solution)/shard_map/ppermute | solution.py:28
  100.4 1.6 %collective-permute-done.12.refs_7_ = bf16[2,256,384]{2,1,0:T(8,128)(2,1)S(1)} collective-permute-done((bf16[2,256,384]{2,1,0:T(8,128)(2,1)S(1)}, bf16[2,256,384]{2,1,0:T(8,128)(2,1)S(1)}, u32[]{:S(2)}, u32[]{:S(2)}) %collective-permute-start.12) | collective-permute-done | bytes 393248 | tf_op jit(solution)/shard_map/ppermute | solution.py:28
  102.1 9.9 %merge.1 = bf16[2,2,2048,128]{3,2,1,0:T(8,128)(2,1)} custom-call(s32[32,16]{1,0:T(8,128)S(1)} %bitcast.31, bf16[2,2048,128]{2,1,0:T(8,128)(2,1)S(1)} %bitcast.30, bf16[7,256,384]{2,1,0:T(8,128)(2,1)S(1)} %constant_dynamic-update-slice_fusion.refs_0_, bf16[3,256,384]{2,1,0:T(8,128)(2,1)S(1)} %collective-permute-done.6.refs_1_, ...), custom_call_target="tpu_custom_call" | custom-call | tf_op jit(solution)/shard_map/merge/pallas_call | solution.py:155
  (18 shorter events, 0.3 us)
Async XLA Ops:
  0.0 10.5 %copy-start.1 = (s32[32,1,16]{0,2,1:T(8,128)S(1)}, s32[32,1,16]{0,2,1:T(8,128)}, u32[]{:S(2)}) copy-start(s32[32,1,16]{0,2,1:T(8,128)} %param.3) | copy-start | bytes 6148
  0.0 32.9 %all-to-all-start = ((bf16[16,256,128]{2,1,0:T(8,128)(2,1)}), bf16[16,256,128]{2,1,0:T(8,128)(2,1)S(1)}, u32[]{:S(2)}, u32[]{:S(2)}) async-start(bf16[16,256,128]{2,1,0:T(8,128)(2,1)} %bitcast.29), calls=%async_computation | async-start | bytes 2097152 | tf_op jit(solution)/shard_map/all_to_all | solution.py:133
  32.9 34.4 %collective-permute-start.5 = (bf16[256,384]{1,0:T(8,128)(2,1)S(1)}, bf16[256,384]{1,0:T(8,128)(2,1)S(1)}, u32[]{:S(2)}, u32[]{:S(2)}) collective-permute-start(bf16[256,384]{1,0:T(8,128)(2,1)S(1)} %pad_maximum_fusion.2), channel_id=1, source_target_pairs={{0,12},{1,13},{2,14},{3,15},{4,8},{5,9},{6,10},{7,11},{8,4},{9,5},... | collective-permute-start | bytes 589832 | tf_op jit(solution)/shard_map/ppermute | solution.py:28
  38.1 29.2 %collective-permute-start.4 = (bf16[256,384]{1,0:T(8,128)(2,1)S(1)}, bf16[256,384]{1,0:T(8,128)(2,1)S(1)}, u32[]{:S(2)}, u32[]{:S(2)}) collective-permute-start(bf16[256,384]{1,0:T(8,128)(2,1)S(1)} %pad_maximum_fusion.2), channel_id=1, source_target_pairs={{0,8},{1,9},{2,10},{3,11},{4,12},{5,13},{6,14},{7,15},{8,0},{9,1},... | collective-permute-start | bytes 589832 | tf_op jit(solution)/shard_map/ppermute | solution.py:28
  42.2 25.0 %collective-permute-start.3 = (bf16[256,384]{1,0:T(8,128)(2,1)S(1)}, bf16[256,384]{1,0:T(8,128)(2,1)S(1)}, u32[]{:S(2)}, u32[]{:S(2)}) collective-permute-start(bf16[256,384]{1,0:T(8,128)(2,1)S(1)} %pad_maximum_fusion.2), channel_id=1, source_target_pairs={{0,3},{1,2},{2,1},{3,0},{4,7},{5,6},{6,5},{7,4},{8,11},{9,10},{10,... | collective-permute-start | bytes 589832 | tf_op jit(solution)/shard_map/ppermute | solution.py:28
  45.4 21.7 %collective-permute-start.2 = (bf16[256,384]{1,0:T(8,128)(2,1)S(1)}, bf16[256,384]{1,0:T(8,128)(2,1)S(1)}, u32[]{:S(2)}, u32[]{:S(2)}) collective-permute-start(bf16[256,384]{1,0:T(8,128)(2,1)S(1)} %pad_maximum_fusion.2), channel_id=1, source_target_pairs={{0,2},{1,3},{2,0},{3,1},{4,6},{5,7},{6,4},{7,5},{8,10},{9,11},{10,... | collective-permute-start | bytes 589832 | tf_op jit(solution)/shard_map/ppermute | solution.py:28
  48.2 11.4 %collective-permute-start = (bf16[256,384]{1,0:T(8,128)(2,1)S(1)}, bf16[256,384]{1,0:T(8,128)(2,1)S(1)}, u32[]{:S(2)}, u32[]{:S(2)}) collective-permute-start(bf16[256,384]{1,0:T(8,128)(2,1)S(1)} %pad_maximum_fusion.2), channel_id=1, source_target_pairs={{0,4},{1,5},{2,6},{3,7},{4,0},{5,1},{6,2},{7,3},{8,12},{9,13},{10,... | collective-permute-start | bytes 589832 | tf_op jit(solution)/shard_map/ppermute | solution.py:28
  59.6 7.5 %collective-permute-start.1 = (bf16[256,384]{1,0:T(8,128)(2,1)S(1)}, bf16[256,384]{1,0:T(8,128)(2,1)S(1)}, u32[]{:S(2)}, u32[]{:S(2)}) collective-permute-start(bf16[256,384]{1,0:T(8,128)(2,1)S(1)} %pad_maximum_fusion.2), channel_id=1, source_target_pairs={{0,1},{1,0},{2,3},{3,2},{4,5},{5,4},{6,7},{7,6},{8,9},{9,8},{10,11... | collective-permute-start | bytes 589832 | tf_op jit(solution)/shard_map/ppermute | solution.py:28
  67.2 34.9 %copy-start = (bf16[2,1,1,2048,128]{4,3,2,1,0:T(8,128)(2,1)S(1)}, bf16[2,1,1,2048,128]{4,3,2,1,0:T(8,128)(2,1)}, u32[]{:S(2)}) copy-start(bf16[2,1,1,2048,128]{4,3,2,1,0:T(8,128)(2,1)} %param.2) | copy-start | bytes 3145732
  67.3 34.7 %collective-permute-start.10 = (bf16[7,256,384]{2,1,0:T(8,128)(2,1)S(1)}, bf16[7,256,384]{2,1,0:T(8,128)(2,1)S(1)}, u32[]{:S(2)}, u32[]{:S(2)}) collective-permute-start(bf16[7,256,384]{2,1,0:T(8,128)(2,1)S(1)} %constant_dynamic-update-slice_fusion.refs_0_), channel_id=1, source_target_pairs={{0,16},{16,0},{32,48},{48,32},{64,80},{80,64},{96,112},{112,96},{1... | collective-permute-start | bytes 4128776 | tf_op jit(solution)/shard_map/ppermute | solution.py:28
  71.2 16.8 %collective-permute-start.6 = (bf16[3,256,384]{2,1,0:T(8,128)(2,1)S(1)}, bf16[3,256,384]{2,1,0:T(8,128)(2,1)S(1)}, u32[]{:S(2)}, u32[]{:S(2)}) collective-permute-start(bf16[3,256,384]{2,1,0:T(8,128)(2,1)S(1)} %pad_maximum_fusion), channel_id=1, source_target_pairs={{0,4},{1,5},{2,6},{3,7},{4,0},{5,1},{6,2},{7,3},{8,12},{9,13},{10,... | collective-permute-start | bytes 1769480 | tf_op jit(solution)/shard_map/ppermute | solution.py:28
  73.2 17.6 %collective-permute-start.9 = (bf16[2,256,384]{2,1,0:T(8,128)(2,1)S(1)}, bf16[2,256,384]{2,1,0:T(8,128)(2,1)S(1)}, u32[]{:S(2)}, u32[]{:S(2)}) collective-permute-start(bf16[2,256,384]{2,1,0:T(8,128)(2,1)S(1)} %pad_maximum_fusion.1), channel_id=1, source_target_pairs={{0,2},{1,3},{2,0},{3,1},{4,6},{5,7},{6,4},{7,5},{8,10},{9,11},{10,... | collective-permute-start | bytes 1179656 | tf_op jit(solution)/shard_map/ppermute | solution.py:28
  78.0 18.1 %collective-permute-start.8 = (bf16[2,256,384]{2,1,0:T(8,128)(2,1)S(1)}, bf16[2,256,384]{2,1,0:T(8,128)(2,1)S(1)}, u32[]{:S(2)}, u32[]{:S(2)}) collective-permute-start(bf16[2,256,384]{2,1,0:T(8,128)(2,1)S(1)} %pad_maximum_fusion.1), channel_id=1, source_target_pairs={{0,3},{1,2},{2,1},{3,0},{4,7},{5,6},{6,5},{7,4},{8,11},{9,10},{10,... | collective-permute-start | bytes 1179656 | tf_op jit(solution)/shard_map/ppermute | solution.py:28
  79.9 18.6 %collective-permute-start.7 = (bf16[2,256,384]{2,1,0:T(8,128)(2,1)S(1)}, bf16[2,256,384]{2,1,0:T(8,128)(2,1)S(1)}, u32[]{:S(2)}, u32[]{:S(2)}) collective-permute-start(bf16[2,256,384]{2,1,0:T(8,128)(2,1)S(1)} %pad_maximum_fusion.1), channel_id=1, source_target_pairs={{0,1},{1,0},{2,3},{3,2},{4,5},{5,4},{6,7},{7,6},{8,9},{9,8},{10,11... | collective-permute-start | bytes 1179656 | tf_op jit(solution)/shard_map/ppermute | solution.py:28
  88.0 14.1 %collective-permute-start.11 = (bf16[3,256,384]{2,1,0:T(8,128)(2,1)S(1)}, bf16[3,256,384]{2,1,0:T(8,128)(2,1)S(1)}, u32[]{:S(2)}, u32[]{:S(2)}) collective-permute-start(bf16[3,256,384]{2,1,0:T(8,128)(2,1)S(1)} %collective-permute-done.6.refs_1_), channel_id=1, source_target_pairs={{0,16},{16,0},{32,48},{48,32},{64,80},{80,64},{96,112},{112,96},{1... | collective-permute-start | bytes 1769480 | tf_op jit(solution)/shard_map/ppermute | solution.py:28
  90.7 9.7 %collective-permute-start.14 = (bf16[2,256,384]{2,1,0:T(8,128)(2,1)S(1)}, bf16[2,256,384]{2,1,0:T(8,128)(2,1)S(1)}, u32[]{:S(2)}, u32[]{:S(2)}) collective-permute-start(bf16[2,256,384]{2,1,0:T(8,128)(2,1)S(1)} %collective-permute-done.9.refs_4_), channel_id=1, source_target_pairs={{0,16},{16,0},{32,48},{48,32},{64,80},{80,64},{96,112},{112,96},{1... | collective-permute-start | bytes 1179656 | tf_op jit(solution)/shard_map/ppermute | solution.py:28
  96.1 4.4 %collective-permute-start.13 = (bf16[2,256,384]{2,1,0:T(8,128)(2,1)S(1)}, bf16[2,256,384]{2,1,0:T(8,128)(2,1)S(1)}, u32[]{:S(2)}, u32[]{:S(2)}) collective-permute-start(bf16[2,256,384]{2,1,0:T(8,128)(2,1)S(1)} %collective-permute-done.8.refs_3_), channel_id=1, source_target_pairs={{0,16},{16,0},{32,48},{48,32},{64,80},{80,64},{96,112},{112,96},{1... | collective-permute-start | bytes 1179656 | tf_op jit(solution)/shard_map/ppermute | solution.py:28
  98.4 3.6 %collective-permute-start.12 = (bf16[2,256,384]{2,1,0:T(8,128)(2,1)S(1)}, bf16[2,256,384]{2,1,0:T(8,128)(2,1)S(1)}, u32[]{:S(2)}, u32[]{:S(2)}) collective-permute-start(bf16[2,256,384]{2,1,0:T(8,128)(2,1)S(1)} %collective-permute-done.7.refs_2_), channel_id=1, source_target_pairs={{0,16},{16,0},{32,48},{48,32},{64,80},{80,64},{96,112},{112,96},{1... | collective-permute-start | bytes 1179656 | tf_op jit(solution)/shard_map/ppermute | solution.py:28
where the time goes:
time: 113 us; the launch traced here: 112 us
  starting transfers between devices  53.8 us (48%)
  waiting for transfers between devices  45 us (40%)
  Pallas kernels  9.89 us (9%)
  between operations  2.21 us (2%)
    ppermute x15, starting transfers between devices, exchange(): return lax.ppermute(block, axis, [(i, i ^ mask) for i in range(count)])  43.3 us
    ppermute x15, waiting for transfers between devices, exchange(): return lax.ppermute(block, axis, [(i, i ^ mask) for i in range(count)])  25.3 us
    all_to_all x1, waiting for transfers between devices, shards(): lax.all_to_all(own_cols.reshape(16, piece, width), 'grp', 0, 0, tiled=True)  19.7 us
    all_to_all x1, starting transfers between devices, shards(): lax.all_to_all(own_cols.reshape(16, piece, width), 'grp', 0, 0, tiled=True)  10.5 us
    pallas_call x1, Pallas kernels, shards(): pl.pallas_call(functools.partial(merge_kernel, points=points, width=width...  9.89 us
  transfers between devices with their start and end apart: 16, of which 6 were waited for; matrix products, arithmetic and copies ran while one was open for 1% of the time, Pallas kernels for 0%

commit v1 on v0

--- a/solution.py
+++ b/solution.py
@@ -17,9 +17,9 @@
     (0, pl.ds(2, 3), 0, pl.ds(1, 3)),
     (0, pl.ds(5, 2), pl.ds(2, 2), 0),
     (1, pl.ds(0, 3), 1, pl.ds(1, 3)),
-    (2, pl.ds(0, 2), pl.ds(2, 2), 1),
-    (3, pl.ds(0, 2), pl.ds(2, 2), 3),
-    (4, pl.ds(0, 2), pl.ds(2, 2), 2),
+    (2, 0, pl.ds(2, 2), 1),
+    (2, 1, pl.ds(2, 2), 3),
+    (2, 2, pl.ds(2, 2), 2),
 )
 
 
@@ -40,7 +40,7 @@
 def merge_kernel(
     order, own_in, *refs, points, width
 ):
-    sides, (out, own, zc, out_v, in_sems, out_sems) = (refs[:5], refs[5:10]), refs[10:]
+    sides, (out, own, zc, out_v, in_sems, out_sems) = (refs[:3], refs[3:6]), refs[6:]
     piece = zc.shape[3]
     me = lax.axis_index("grp")
     box = lax.axis_index("box")
@@ -98,26 +98,24 @@
     echo = stacked(times(zs, v).astype(jnp.bfloat16), width)
 
     sent = []
-    for xk in range(4):
+    for side, right in ((1, resp), (0, echo)):
+        half = jnp.bitwise_xor(parity, side)
         for zl in range(2):
-            m = jnp.bitwise_xor(x, xk) + 4 * jnp.bitwise_xor(z_low, zl)
-            rows = pl.ds(pl.multiple_of(m * piece, piece), piece)
-            for side, right in ((0, echo), (1, resp)):
-                zr = zc[side, zl + 2 * z_high, xk]
-                zi = zc[side, zl + 2 - 2 * z_high, xk]
-                acc = dot(jnp.concatenate([zr, zi], axis=1), right)
-                half = jnp.bitwise_xor(parity, side)
+            zr = zc[side, zl + 2 * z_high].reshape(4 * piece, IFACE)
+            zi = zc[side, zl + 2 - 2 * z_high].reshape(4 * piece, IFACE)
+            acc = dot(jnp.concatenate([zr, zi], axis=1), right)
+            for xk in range(4):
+                m = jnp.bitwise_xor(x, xk) + 4 * jnp.bitwise_xor(z_low, zl)
+                rows = pl.ds(pl.multiple_of(m * piece, piece), piece)
                 for p in range(2):
-                    val = acc[:, p * width : (p + 1) * width]
+                    val = acc[xk * piece : (xk + 1) * piece, p * width : (p + 1) * width]
                     if side == 0:
                         val = own[p, rows, :].astype(jnp.float32) * ext + val * (1.0 / points)
                     else:
                         val = val * -(points ** -0.5)
                     out_v[p, half, rows, :] = val.astype(jnp.bfloat16)
                 view = (slice(None), half, rows)
-                c = pltpu.make_async_copy(
-                    out_v.at[view], out.at[view], out_sems.at[len(sent)]
-                )
+                c = pltpu.make_async_copy(out_v.at[view], out.at[view], out_sems.at[len(sent)])
                 c.start()
                 sent.append(c)
     for c in sent:
@@ -147,21 +145,21 @@
     near = jnp.stack([x1, x2, x3])
     far = jnp.stack([z2, z3])
     every = jnp.stack([mine, z1, x1, x2, x3, z2, z3])
-    late = [exchange(near, "grp", 4)]
-    late += [exchange(far, "grp", k) for k in (1, 3, 2)]
-    gathered = [every] + late
+    beside = exchange(near, "grp", 4)
+    both = jnp.stack([exchange(far, "grp", k) for k in (1, 3, 2)])
+    gathered = [every, beside, both]
     gathered += [exchange(g, "box", 1) for g in gathered]
     anywhere = pl.BlockSpec(memory_space=pl.ANY)
     out = pl.pallas_call(
         functools.partial(merge_kernel, points=points, width=width),
         out_shape=jax.ShapeDtypeStruct((2, 2, points, width), jnp.bfloat16),
-        in_specs=[pl.BlockSpec(memory_space=pltpu.SMEM)] + [anywhere] * 11,
+        in_specs=[pl.BlockSpec(memory_space=pltpu.SMEM)] + [anywhere] * 7,
         out_specs=anywhere,
         scratch_shapes=[
             pltpu.VMEM((2, points, width), jnp.bfloat16),
             pltpu.VMEM((2, 4, 4, piece, IFACE), jnp.bfloat16),
             pltpu.VMEM((2, 2, points, width), jnp.bfloat16),
-            pltpu.SemaphoreType.DMA((17,)),
+            pltpu.SemaphoreType.DMA((15,)),
             pltpu.SemaphoreType.DMA((16,)),
         ],
         compiler_params=pltpu.CompilerParams(vmem_limit_bytes=24 << 20),

time: 113 us -> 101 us (0.89)
  waiting for transfers between devices: 45 us -> 34.8 us
    ppermute x15 -> x13, waiting for transfers between devices: 25.3 us -> 15.2 us  [exchange(): return lax.ppermute(block, axis, [(i, i ^ mask) for i in range(count)])]
    ppermute x15 -> x13, starting transfers between devices: 43.3 us -> 42.4 us  [exchange(): return lax.ppermute(block, axis, [(i, i ^ mask) for i in range(count)])]
  transfers between devices with their start and end apart: 16 -> 14, of which waited for: 6 -> 5; matrix products, arithmetic and copies ran while one was open for 1% -> 1% of each run, Pallas kernels for 0% -> 0%
where the time goes in v1:
time: 101 us
  starting transfers between devices  52.9 us (52%)
  waiting for transfers between devices  34.8 us (34%)
  Pallas kernels  9.48 us (9%)
  between operations  2.24 us (2%)
    ppermute x13, starting transfers between devices, exchange(): return lax.ppermute(block, axis, [(i, i ^ mask) for i in range(count)])  42.4 us
    all_to_all x1, waiting for transfers between devices, shards(): lax.all_to_all(own_cols.reshape(16, piece, width), 'grp', 0, 0, tiled=True)  19.6 us
    ppermute x13, waiting for transfers between devices, exchange(): return lax.ppermute(block, axis, [(i, i ^ mask) for i in range(count)])  15.2 us
    all_to_all x1, starting transfers between devices, shards(): lax.all_to_all(own_cols.reshape(16, piece, width), 'grp', 0, 0, tiled=True)  10.5 us
    pallas_call x1, Pallas kernels, shards(): pl.pallas_call(functools.partial(merge_kernel, points=points, width=width...  9.48 us
  transfers between devices with their start and end apart: 14, of which 5 were waited for; matrix products, arithmetic and copies ran while one was open for 1% of the time, Pallas kernels for 0%

profile of v1, /device:TPU:1, one launch (start us, length us, event | category | flops | bytes accessed | tf_op | source)
XLA Modules:
  0.0 100.7 jit_solution(2906782935726129763)
XLA Ops:
  0.0 10.5 %all-to-all-start = ((bf16[16,256,128]{2,1,0:T(8,128)(2,1)}), bf16[16,256,128]{2,1,0:T(8,128)(2,1)S(1)}, u32[]{:S(2)}, u32[]{:S(2)}) async-start(bf16[16,256,128]{2,1,0:T(8,128)(2,1)} %bitcast.32), calls=%async_computation | async-start | bytes 2097152 | tf_op jit(solution)/shard_map/all_to_all | solution.py:131
  10.5 0.7 constant_dynamic-slice_fusion.1
  13.2 0.1 copy.3
  13.2 19.6 %all-to-all-done = bf16[16,256,128]{2,1,0:T(8,128)(2,1)S(1)} async-done(((bf16[16,256,128]{2,1,0:T(8,128)(2,1)}), bf16[16,256,128]{2,1,0:T(8,128)(2,1)S(1)}, u32[]{:S(2)}, u32[]{:S(2)}) %all-to-all-start) | async-done | bytes 1048608 | tf_op jit(solution)/shard_map/all_to_all | solution.py:131
  32.9 5.1 %collective-permute-start.5 = (bf16[256,384]{1,0:T(8,128)(2,1)S(1)}, bf16[256,384]{1,0:T(8,128)(2,1)S(1)}, u32[]{:S(2)}, u32[]{:S(2)}) collective-permute-start(bf16[256,384]{1,0:T(8,128)(2,1)S(1)} %pad_maximum_fusion.3), channel_id=1, source_target_pairs={{0,12},{1,13},{2,14},{3,15},{4,8},{5,9},{6,10},{7,11},{8,4},{9,5},... | collective-permute-start | bytes 589832 | tf_op jit(solution)/shard_map/ppermute | solution.py:28
  38.1 4.1 %collective-permute-start.4 = (bf16[256,384]{1,0:T(8,128)(2,1)S(1)}, bf16[256,384]{1,0:T(8,128)(2,1)S(1)}, u32[]{:S(2)}, u32[]{:S(2)}) collective-permute-start(bf16[256,384]{1,0:T(8,128)(2,1)S(1)} %pad_maximum_fusion.3), channel_id=1, source_target_pairs={{0,8},{1,9},{2,10},{3,11},{4,12},{5,13},{6,14},{7,15},{8,0},{9,1},... | collective-permute-start | bytes 589832 | tf_op jit(solution)/shard_map/ppermute | solution.py:28
  42.2 3.2 %collective-permute-start.3 = (bf16[256,384]{1,0:T(8,128)(2,1)S(1)}, bf16[256,384]{1,0:T(8,128)(2,1)S(1)}, u32[]{:S(2)}, u32[]{:S(2)}) collective-permute-start(bf16[256,384]{1,0:T(8,128)(2,1)S(1)} %pad_maximum_fusion.3), channel_id=1, source_target_pairs={{0,3},{1,2},{2,1},{3,0},{4,7},{5,6},{6,5},{7,4},{8,11},{9,10},{10,... | collective-permute-start | bytes 589832 | tf_op jit(solution)/shard_map/ppermute | solution.py:28
  45.4 2.8 %collective-permute-start.2 = (bf16[256,384]{1,0:T(8,128)(2,1)S(1)}, bf16[256,384]{1,0:T(8,128)(2,1)S(1)}, u32[]{:S(2)}, u32[]{:S(2)}) collective-permute-start(bf16[256,384]{1,0:T(8,128)(2,1)S(1)} %pad_maximum_fusion.3), channel_id=1, source_target_pairs={{0,2},{1,3},{2,0},{3,1},{4,6},{5,7},{6,4},{7,5},{8,10},{9,11},{10,... | collective-permute-start | bytes 589832 | tf_op jit(solution)/shard_map/ppermute | solution.py:28
  48.2 2.0 %collective-permute-start = (bf16[256,384]{1,0:T(8,128)(2,1)S(1)}, bf16[256,384]{1,0:T(8,128)(2,1)S(1)}, u32[]{:S(2)}, u32[]{:S(2)}) collective-permute-start(bf16[256,384]{1,0:T(8,128)(2,1)S(1)} %pad_maximum_fusion.3), channel_id=1, source_target_pairs={{0,4},{1,5},{2,6},{3,7},{4,0},{5,1},{6,2},{7,3},{8,12},{9,13},{10,... | collective-permute-start | bytes 589832 | tf_op jit(solution)/shard_map/ppermute | solution.py:28
  50.3 0.0 collective-permute-done.5
  50.3 3.1 %collective-permute-start.1 = (bf16[256,384]{1,0:T(8,128)(2,1)S(1)}, bf16[256,384]{1,0:T(8,128)(2,1)S(1)}, u32[]{:S(2)}, u32[]{:S(2)}) collective-permute-start(bf16[256,384]{1,0:T(8,128)(2,1)S(1)} %pad_maximum_fusion.3), channel_id=1, source_target_pairs={{0,1},{1,0},{2,3},{3,2},{4,5},{5,4},{6,7},{7,6},{8,9},{9,8},{10,11... | collective-permute-start | bytes 589832 | tf_op jit(solution)/shard_map/ppermute | solution.py:28
  53.4 1.3 %collective-permute-done.4 = bf16[256,384]{1,0:T(8,128)(2,1)S(1)} collective-permute-done((bf16[256,384]{1,0:T(8,128)(2,1)S(1)}, bf16[256,384]{1,0:T(8,128)(2,1)S(1)}, u32[]{:S(2)}, u32[]{:S(2)}) %collective-permute-start.4) | collective-permute-done | bytes 196640 | tf_op jit(solution)/shard_map/ppermute | solution.py:28
  54.8 6.0 %collective-permute-start.9 = (bf16[2,256,384]{2,1,0:T(8,128)(2,1)S(1)}, bf16[2,256,384]{2,1,0:T(8,128)(2,1)S(1)}, u32[]{:S(2)}, u32[]{:S(2)}) collective-permute-start(bf16[2,256,384]{2,1,0:T(8,128)(2,1)S(1)} %pad_maximum_fusion.2), channel_id=1, source_target_pairs={{0,2},{1,3},{2,0},{3,1},{4,6},{5,7},{6,4},{7,5},{8,10},{9,11},{10,... | collective-permute-start | bytes 1179656 | tf_op jit(solution)/shard_map/ppermute | solution.py:28
  60.8 3.3 %collective-permute-start.8 = (bf16[2,256,384]{2,1,0:T(8,128)(2,1)S(1)}, bf16[2,256,384]{2,1,0:T(8,128)(2,1)S(1)}, u32[]{:S(2)}, u32[]{:S(2)}) collective-permute-start(bf16[2,256,384]{2,1,0:T(8,128)(2,1)S(1)} %pad_maximum_fusion.2), channel_id=1, source_target_pairs={{0,3},{1,2},{2,1},{3,0},{4,7},{5,6},{6,5},{7,4},{8,11},{9,10},{10,... | collective-permute-start | bytes 1179656 | tf_op jit(solution)/shard_map/ppermute | solution.py:28
  64.1 0.0 collective-permute-done.1
  64.1 1.9 %collective-permute-start.7 = (bf16[2,256,384]{2,1,0:T(8,128)(2,1)S(1)}, bf16[2,256,384]{2,1,0:T(8,128)(2,1)S(1)}, u32[]{:S(2)}, u32[]{:S(2)}) collective-permute-start(bf16[2,256,384]{2,1,0:T(8,128)(2,1)S(1)} %pad_maximum_fusion.2), channel_id=1, source_target_pairs={{0,1},{1,0},{2,3},{3,2},{4,5},{5,4},{6,7},{7,6},{8,9},{9,8},{10,11... | collective-permute-start | bytes 1179656 | tf_op jit(solution)/shard_map/ppermute | solution.py:28
  66.1 0.0 collective-permute-done.2
  66.2 0.0 collective-permute-done.3
  66.3 3.5 %collective-permute-start.10 = (bf16[7,256,384]{2,1,0:T(8,128)(2,1)S(1)}, bf16[7,256,384]{2,1,0:T(8,128)(2,1)S(1)}, u32[]{:S(2)}, u32[]{:S(2)}) collective-permute-start(bf16[7,256,384]{2,1,0:T(8,128)(2,1)S(1)} %constant_dynamic-update-slice_fusion.refs_0_), channel_id=1, source_target_pairs={{0,16},{16,0},{32,48},{48,32},{64,80},{80,64},{96,112},{112,96},{1... | collective-permute-start | bytes 4128776 | tf_op jit(solution)/shard_map/ppermute | solution.py:28
  69.8 0.1 pad_maximum_fusion.1
  69.9 0.0 copy-start
  69.9 2.1 %collective-permute-start.6 = (bf16[3,256,384]{2,1,0:T(8,128)(2,1)S(1)}, bf16[3,256,384]{2,1,0:T(8,128)(2,1)S(1)}, u32[]{:S(2)}, u32[]{:S(2)}) collective-permute-start(bf16[3,256,384]{2,1,0:T(8,128)(2,1)S(1)} %pad_maximum_fusion.1), channel_id=1, source_target_pairs={{0,4},{1,5},{2,6},{3,7},{4,0},{5,1},{6,2},{7,3},{8,12},{9,13},{10,... | collective-permute-start | bytes 1769480 | tf_op jit(solution)/shard_map/ppermute | solution.py:28
  72.0 0.0 collective-permute-done.9
  72.0 7.0 %collective-permute-done.8 = bf16[2,256,384]{2,1,0:T(8,128)(2,1)S(1)} collective-permute-done((bf16[2,256,384]{2,1,0:T(8,128)(2,1)S(1)}, bf16[2,256,384]{2,1,0:T(8,128)(2,1)S(1)}, u32[]{:S(2)}, u32[]{:S(2)}) %collective-permute-start.8) | collective-permute-done | bytes 393248 | tf_op jit(solution)/shard_map/ppermute | solution.py:28
  79.0 0.0 collective-permute-done.7
  79.0 0.2 pad_maximum_fusion.refs_2_
  79.1 2.4 %collective-permute-start.12 = (bf16[3,2,256,384]{3,2,1,0:T(8,128)(2,1)S(1)}, bf16[3,2,256,384]{3,2,1,0:T(8,128)(2,1)S(1)}, u32[]{:S(2)}, u32[]{:S(2)}) collective-permute-start(bf16[3,2,256,384]{3,2,1,0:T(8,128)(2,1)S(1)} %pad_maximum_fusion.refs_2_), channel_id=1, source_target_pairs={{0,16},{16,0},{32,48},{48,32},{64,80},{80,64},{96,112},{112,96},{1... | collective-permute-start | bytes 3538952 | tf_op jit(solution)/shard_map/ppermute | solution.py:28
  81.5 5.3 %collective-permute-done.6.refs_1_ = bf16[3,256,384]{2,1,0:T(8,128)(2,1)S(1)} collective-permute-done((bf16[3,256,384]{2,1,0:T(8,128)(2,1)S(1)}, bf16[3,256,384]{2,1,0:T(8,128)(2,1)S(1)}, u32[]{:S(2)}, u32[]{:S(2)}) %collective-permute-start.6) | collective-permute-done | bytes 589856 | tf_op jit(solution)/shard_map/ppermute | solution.py:28
  86.8 2.8 %collective-permute-start.11 = (bf16[3,256,384]{2,1,0:T(8,128)(2,1)S(1)}, bf16[3,256,384]{2,1,0:T(8,128)(2,1)S(1)}, u32[]{:S(2)}, u32[]{:S(2)}) collective-permute-start(bf16[3,256,384]{2,1,0:T(8,128)(2,1)S(1)} %collective-permute-done.6.refs_1_), channel_id=1, source_target_pairs={{0,16},{16,0},{32,48},{48,32},{64,80},{80,64},{96,112},{112,96},{1... | collective-permute-start | bytes 1769480 | tf_op jit(solution)/shard_map/ppermute | solution.py:28
  89.6 1.6 %collective-permute-done.11.refs_4_ = bf16[3,256,384]{2,1,0:T(8,128)(2,1)S(1)} collective-permute-done((bf16[3,256,384]{2,1,0:T(8,128)(2,1)S(1)}, bf16[3,256,384]{2,1,0:T(8,128)(2,1)S(1)}, u32[]{:S(2)}, u32[]{:S(2)}) %collective-permute-start.11) | collective-permute-done | bytes 589856 | tf_op jit(solution)/shard_map/ppermute | solution.py:28
  91.2 0.0 collective-permute-done.10.refs_3_
  91.2 9.5 %merge.1 = bf16[2,2,2048,128]{3,2,1,0:T(8,128)(2,1)} custom-call(s32[32,16]{1,0:T(8,128)S(1)} %bitcast.34, bf16[2,2048,128]{2,1,0:T(8,128)(2,1)S(1)} %bitcast.33, bf16[7,256,384]{2,1,0:T(8,128)(2,1)S(1)} %constant_dynamic-update-slice_fusion.refs_0_, bf16[3,256,384]{2,1,0:T(8,128)(2,1)S(1)} %collective-permute-done.6.refs_1_, ...), custom_call_target="tpu_custom_call" | custom-call | tf_op jit(solution)/shard_map/merge/pallas_call | solution.py:153
  (15 shorter events, 0.3 us)
Async XLA Ops:
  0.0 10.5 %copy-start.1 = (s32[32,1,16]{0,2,1:T(8,128)S(1)}, s32[32,1,16]{0,2,1:T(8,128)}, u32[]{:S(2)}) copy-start(s32[32,1,16]{0,2,1:T(8,128)} %param.3) | copy-start | bytes 6148
  0.0 32.9 %all-to-all-start = ((bf16[16,256,128]{2,1,0:T(8,128)(2,1)}), bf16[16,256,128]{2,1,0:T(8,128)(2,1)S(1)}, u32[]{:S(2)}, u32[]{:S(2)}) async-start(bf16[16,256,128]{2,1,0:T(8,128)(2,1)} %bitcast.32), calls=%async_computation | async-start | bytes 2097152 | tf_op jit(solution)/shard_map/all_to_all | solution.py:131
  32.9 17.4 %collective-permute-start.5 = (bf16[256,384]{1,0:T(8,128)(2,1)S(1)}, bf16[256,384]{1,0:T(8,128)(2,1)S(1)}, u32[]{:S(2)}, u32[]{:S(2)}) collective-permute-start(bf16[256,384]{1,0:T(8,128)(2,1)S(1)} %pad_maximum_fusion.3), channel_id=1, source_target_pairs={{0,12},{1,13},{2,14},{3,15},{4,8},{5,9},{6,10},{7,11},{8,4},{9,5},... | collective-permute-start | bytes 589832 | tf_op jit(solution)/shard_map/ppermute | solution.py:28
  38.1 16.7 %collective-permute-start.4 = (bf16[256,384]{1,0:T(8,128)(2,1)S(1)}, bf16[256,384]{1,0:T(8,128)(2,1)S(1)}, u32[]{:S(2)}, u32[]{:S(2)}) collective-permute-start(bf16[256,384]{1,0:T(8,128)(2,1)S(1)} %pad_maximum_fusion.3), channel_id=1, source_target_pairs={{0,8},{1,9},{2,10},{3,11},{4,12},{5,13},{6,14},{7,15},{8,0},{9,1},... | collective-permute-start | bytes 589832 | tf_op jit(solution)/shard_map/ppermute | solution.py:28
  42.2 24.0 %collective-permute-start.3 = (bf16[256,384]{1,0:T(8,128)(2,1)S(1)}, bf16[256,384]{1,0:T(8,128)(2,1)S(1)}, u32[]{:S(2)}, u32[]{:S(2)}) collective-permute-start(bf16[256,384]{1,0:T(8,128)(2,1)S(1)} %pad_maximum_fusion.3), channel_id=1, source_target_pairs={{0,3},{1,2},{2,1},{3,0},{4,7},{5,6},{6,5},{7,4},{8,11},{9,10},{10,... | collective-permute-start | bytes 589832 | tf_op jit(solution)/shard_map/ppermute | solution.py:28
  45.4 20.7 %collective-permute-start.2 = (bf16[256,384]{1,0:T(8,128)(2,1)S(1)}, bf16[256,384]{1,0:T(8,128)(2,1)S(1)}, u32[]{:S(2)}, u32[]{:S(2)}) collective-permute-start(bf16[256,384]{1,0:T(8,128)(2,1)S(1)} %pad_maximum_fusion.3), channel_id=1, source_target_pairs={{0,2},{1,3},{2,0},{3,1},{4,6},{5,7},{6,4},{7,5},{8,10},{9,11},{10,... | collective-permute-start | bytes 589832 | tf_op jit(solution)/shard_map/ppermute | solution.py:28
  48.2 12.6 %collective-permute-start = (bf16[256,384]{1,0:T(8,128)(2,1)S(1)}, bf16[256,384]{1,0:T(8,128)(2,1)S(1)}, u32[]{:S(2)}, u32[]{:S(2)}) collective-permute-start(bf16[256,384]{1,0:T(8,128)(2,1)S(1)} %pad_maximum_fusion.3), channel_id=1, source_target_pairs={{0,4},{1,5},{2,6},{3,7},{4,0},{5,1},{6,2},{7,3},{8,12},{9,13},{10,... | collective-permute-start | bytes 589832 | tf_op jit(solution)/shard_map/ppermute | solution.py:28
  50.3 13.8 %collective-permute-start.1 = (bf16[256,384]{1,0:T(8,128)(2,1)S(1)}, bf16[256,384]{1,0:T(8,128)(2,1)S(1)}, u32[]{:S(2)}, u32[]{:S(2)}) collective-permute-start(bf16[256,384]{1,0:T(8,128)(2,1)S(1)} %pad_maximum_fusion.3), channel_id=1, source_target_pairs={{0,1},{1,0},{2,3},{3,2},{4,5},{5,4},{6,7},{7,6},{8,9},{9,8},{10,11... | collective-permute-start | bytes 589832 | tf_op jit(solution)/shard_map/ppermute | solution.py:28
  54.8 17.2 %collective-permute-start.9 = (bf16[2,256,384]{2,1,0:T(8,128)(2,1)S(1)}, bf16[2,256,384]{2,1,0:T(8,128)(2,1)S(1)}, u32[]{:S(2)}, u32[]{:S(2)}) collective-permute-start(bf16[2,256,384]{2,1,0:T(8,128)(2,1)S(1)} %pad_maximum_fusion.2), channel_id=1, source_target_pairs={{0,2},{1,3},{2,0},{3,1},{4,6},{5,7},{6,4},{7,5},{8,10},{9,11},{10,... | collective-permute-start | bytes 1179656 | tf_op jit(solution)/shard_map/ppermute | solution.py:28
  60.8 18.2 %collective-permute-start.8 = (bf16[2,256,384]{2,1,0:T(8,128)(2,1)S(1)}, bf16[2,256,384]{2,1,0:T(8,128)(2,1)S(1)}, u32[]{:S(2)}, u32[]{:S(2)}) collective-permute-start(bf16[2,256,384]{2,1,0:T(8,128)(2,1)S(1)} %pad_maximum_fusion.2), channel_id=1, source_target_pairs={{0,3},{1,2},{2,1},{3,0},{4,7},{5,6},{6,5},{7,4},{8,11},{9,10},{10,... | collective-permute-start | bytes 1179656 | tf_op jit(solution)/shard_map/ppermute | solution.py:28
  64.1 14.8 %collective-permute-start.7 = (bf16[2,256,384]{2,1,0:T(8,128)(2,1)S(1)}, bf16[2,256,384]{2,1,0:T(8,128)(2,1)S(1)}, u32[]{:S(2)}, u32[]{:S(2)}) collective-permute-start(bf16[2,256,384]{2,1,0:T(8,128)(2,1)S(1)} %pad_maximum_fusion.2), channel_id=1, source_target_pairs={{0,1},{1,0},{2,3},{3,2},{4,5},{5,4},{6,7},{7,6},{8,9},{9,8},{10,11... | collective-permute-start | bytes 1179656 | tf_op jit(solution)/shard_map/ppermute | solution.py:28
  66.3 24.9 %collective-permute-start.10 = (bf16[7,256,384]{2,1,0:T(8,128)(2,1)S(1)}, bf16[7,256,384]{2,1,0:T(8,128)(2,1)S(1)}, u32[]{:S(2)}, u32[]{:S(2)}) collective-permute-start(bf16[7,256,384]{2,1,0:T(8,128)(2,1)S(1)} %constant_dynamic-update-slice_fusion.refs_0_), channel_id=1, source_target_pairs={{0,16},{16,0},{32,48},{48,32},{64,80},{80,64},{96,112},{112,96},{1... | collective-permute-start | bytes 4128776 | tf_op jit(solution)/shard_map/ppermute | solution.py:28
  69.9 21.3 %copy-start = (bf16[2,1,1,2048,128]{4,3,2,1,0:T(8,128)(2,1)S(1)}, bf16[2,1,1,2048,128]{4,3,2,1,0:T(8,128)(2,1)}, u32[]{:S(2)}) copy-start(bf16[2,1,1,2048,128]{4,3,2,1,0:T(8,128)(2,1)} %param.2) | copy-start | bytes 3145732
  69.9 16.9 %collective-permute-start.6 = (bf16[3,256,384]{2,1,0:T(8,128)(2,1)S(1)}, bf16[3,256,384]{2,1,0:T(8,128)(2,1)S(1)}, u32[]{:S(2)}, u32[]{:S(2)}) collective-permute-start(bf16[3,256,384]{2,1,0:T(8,128)(2,1)S(1)} %pad_maximum_fusion.1), channel_id=1, source_target_pairs={{0,4},{1,5},{2,6},{3,7},{4,0},{5,1},{6,2},{7,3},{8,12},{9,13},{10,... | collective-permute-start | bytes 1769480 | tf_op jit(solution)/shard_map/ppermute | solution.py:28
  79.1 12.1 %collective-permute-start.12 = (bf16[3,2,256,384]{3,2,1,0:T(8,128)(2,1)S(1)}, bf16[3,2,256,384]{3,2,1,0:T(8,128)(2,1)S(1)}, u32[]{:S(2)}, u32[]{:S(2)}) collective-permute-start(bf16[3,2,256,384]{3,2,1,0:T(8,128)(2,1)S(1)} %pad_maximum_fusion.refs_2_), channel_id=1, source_target_pairs={{0,16},{16,0},{32,48},{48,32},{64,80},{80,64},{96,112},{112,96},{1... | collective-permute-start | bytes 3538952 | tf_op jit(solution)/shard_map/ppermute | solution.py:28
  86.8 4.4 %collective-permute-start.11 = (bf16[3,256,384]{2,1,0:T(8,128)(2,1)S(1)}, bf16[3,256,384]{2,1,0:T(8,128)(2,1)S(1)}, u32[]{:S(2)}, u32[]{:S(2)}) collective-permute-start(bf16[3,256,384]{2,1,0:T(8,128)(2,1)S(1)} %collective-permute-done.6.refs_1_), channel_id=1, source_target_pairs={{0,16},{16,0},{32,48},{48,32},{64,80},{80,64},{96,112},{112,96},{1... | collective-permute-start | bytes 1769480 | tf_op jit(solution)/shard_map/ppermute | solution.py:28

commit v2 on v1

--- a/solution.py
+++ b/solution.py
@@ -17,9 +17,9 @@
     (0, pl.ds(2, 3), 0, pl.ds(1, 3)),
     (0, pl.ds(5, 2), pl.ds(2, 2), 0),
     (1, pl.ds(0, 3), 1, pl.ds(1, 3)),
-    (2, 0, pl.ds(2, 2), 1),
-    (2, 1, pl.ds(2, 2), 3),
-    (2, 2, pl.ds(2, 2), 2),
+    (1, pl.ds(3, 2), pl.ds(2, 2), 1),
+    (1, pl.ds(5, 2), pl.ds(2, 2), 3),
+    (1, pl.ds(7, 2), pl.ds(2, 2), 2),
 )
 
 
@@ -40,7 +40,7 @@
 def merge_kernel(
     order, own_in, *refs, points, width
 ):
-    sides, (out, own, zc, out_v, in_sems, out_sems) = (refs[:3], refs[3:6]), refs[6:]
+    sides, (out, own, zc, out_v, in_sems, out_sems) = (refs[:2], refs[2:4]), refs[4:]
     piece = zc.shape[3]
     me = lax.axis_index("grp")
     box = lax.axis_index("box")
@@ -145,15 +145,15 @@
     near = jnp.stack([x1, x2, x3])
     far = jnp.stack([z2, z3])
     every = jnp.stack([mine, z1, x1, x2, x3, z2, z3])
-    beside = exchange(near, "grp", 4)
-    both = jnp.stack([exchange(far, "grp", k) for k in (1, 3, 2)])
-    gathered = [every, beside, both]
+    late = [exchange(near, "grp", 4)]
+    late += [exchange(far, "grp", k) for k in (1, 3, 2)]
+    gathered = [every, jnp.concatenate(late, axis=0)]
     gathered += [exchange(g, "box", 1) for g in gathered]
     anywhere = pl.BlockSpec(memory_space=pl.ANY)
     out = pl.pallas_call(
         functools.partial(merge_kernel, points=points, width=width),
         out_shape=jax.ShapeDtypeStruct((2, 2, points, width), jnp.bfloat16),
-        in_specs=[pl.BlockSpec(memory_space=pltpu.SMEM)] + [anywhere] * 7,
+        in_specs=[pl.BlockSpec(memory_space=pltpu.SMEM)] + [anywhere] * 5,
         out_specs=anywhere,
         scratch_shapes=[
             pltpu.VMEM((2, points, width), jnp.bfloat16),

time: 101 us -> 100 us (0.990)
  starting transfers between devices: 52.9 us -> 49 us
  waiting for transfers between devices: 34.8 us -> 37.3 us
    ppermute x13 -> x12, starting transfers between devices: 42.4 us -> 38.5 us  [exchange(): return lax.ppermute(block, axis, [(i, i ^ mask) for i in range(count)])]
    ppermute x13 -> x12, waiting for transfers between devices: 15.2 us -> 17.7 us  [exchange(): return lax.ppermute(block, axis, [(i, i ^ mask) for i in range(count)])]
  transfers between devices with their start and end apart: 14 -> 13, of which waited for: 5 -> 4; matrix products, arithmetic and copies ran while one was open for 1% -> 1% of each run, Pallas kernels for 0% -> 0%
where the time goes in v2:
time: 100 us; the launch traced here: 99.5 us
  starting transfers between devices  49 us (49%)
  waiting for transfers between devices  37.3 us (37%)
  Pallas kernels  9.48 us (9%)
  between operations  2.26 us (2%)
  local copies, waits for them, and re-layouts  1.25 us (1%)
    ppermute x12, starting transfers between devices, exchange(): return lax.ppermute(block, axis, [(i, i ^ mask) for i in range(count)])  38.5 us
    all_to_all x1, waiting for transfers between devices, shards(): lax.all_to_all(own_cols.reshape(16, piece, width), 'grp', 0, 0, tiled=True)  19.6 us
    ppermute x12, waiting for transfers between devices, exchange(): return lax.ppermute(block, axis, [(i, i ^ mask) for i in range(count)])  17.7 us
    all_to_all x1, starting transfers between devices, shards(): lax.all_to_all(own_cols.reshape(16, piece, width), 'grp', 0, 0, tiled=True)  10.5 us
    pallas_call x1, Pallas kernels, shards(): pl.pallas_call(functools.partial(merge_kernel, points=points, width=width...  9.48 us
  transfers between devices with their start and end apart: 13, of which 4 were waited for; matrix products, arithmetic and copies ran while one was open for 1% of the time, Pallas kernels for 0%

profile of v2, /device:TPU:1, one launch (start us, length us, event | category | flops | bytes accessed | tf_op | source)
XLA Modules:
  0.0 99.5 jit_solution(10696322838719855673)
XLA Ops:
  0.0 10.5 %all-to-all-start = ((bf16[16,256,128]{2,1,0:T(8,128)(2,1)}), bf16[16,256,128]{2,1,0:T(8,128)(2,1)S(1)}, u32[]{:S(2)}, u32[]{:S(2)}) async-start(bf16[16,256,128]{2,1,0:T(8,128)(2,1)} %bitcast.29), calls=%async_computation | async-start | bytes 2097152 | tf_op jit(solution)/shard_map/all_to_all | solution.py:131
  10.5 0.7 constant_dynamic-slice_fusion.1
  13.2 0.1 copy.3
  13.2 19.6 %all-to-all-done = bf16[16,256,128]{2,1,0:T(8,128)(2,1)S(1)} async-done(((bf16[16,256,128]{2,1,0:T(8,128)(2,1)}), bf16[16,256,128]{2,1,0:T(8,128)(2,1)S(1)}, u32[]{:S(2)}, u32[]{:S(2)}) %all-to-all-start) | async-done | bytes 1048608 | tf_op jit(solution)/shard_map/all_to_all | solution.py:131
  32.9 5.1 %collective-permute-start.5 = (bf16[256,384]{1,0:T(8,128)(2,1)S(1)}, bf16[256,384]{1,0:T(8,128)(2,1)S(1)}, u32[]{:S(2)}, u32[]{:S(2)}) collective-permute-start(bf16[256,384]{1,0:T(8,128)(2,1)S(1)} %pad_maximum_fusion.2), channel_id=1, source_target_pairs={{0,12},{1,13},{2,14},{3,15},{4,8},{5,9},{6,10},{7,11},{8,4},{9,5},... | collective-permute-start | bytes 589832 | tf_op jit(solution)/shard_map/ppermute | solution.py:28
  38.1 4.1 %collective-permute-start.4 = (bf16[256,384]{1,0:T(8,128)(2,1)S(1)}, bf16[256,384]{1,0:T(8,128)(2,1)S(1)}, u32[]{:S(2)}, u32[]{:S(2)}) collective-permute-start(bf16[256,384]{1,0:T(8,128)(2,1)S(1)} %pad_maximum_fusion.2), channel_id=1, source_target_pairs={{0,8},{1,9},{2,10},{3,11},{4,12},{5,13},{6,14},{7,15},{8,0},{9,1},... | collective-permute-start | bytes 589832 | tf_op jit(solution)/shard_map/ppermute | solution.py:28
  42.2 3.2 %collective-permute-start.3 = (bf16[256,384]{1,0:T(8,128)(2,1)S(1)}, bf16[256,384]{1,0:T(8,128)(2,1)S(1)}, u32[]{:S(2)}, u32[]{:S(2)}) collective-permute-start(bf16[256,384]{1,0:T(8,128)(2,1)S(1)} %pad_maximum_fusion.2), channel_id=1, source_target_pairs={{0,3},{1,2},{2,1},{3,0},{4,7},{5,6},{6,5},{7,4},{8,11},{9,10},{10,... | collective-permute-start | bytes 589832 | tf_op jit(solution)/shard_map/ppermute | solution.py:28
  45.4 2.8 %collective-permute-start.2 = (bf16[256,384]{1,0:T(8,128)(2,1)S(1)}, bf16[256,384]{1,0:T(8,128)(2,1)S(1)}, u32[]{:S(2)}, u32[]{:S(2)}) collective-permute-start(bf16[256,384]{1,0:T(8,128)(2,1)S(1)} %pad_maximum_fusion.2), channel_id=1, source_target_pairs={{0,2},{1,3},{2,0},{3,1},{4,6},{5,7},{6,4},{7,5},{8,10},{9,11},{10,... | collective-permute-start | bytes 589832 | tf_op jit(solution)/shard_map/ppermute | solution.py:28
  48.2 2.9 %collective-permute-start.1 = (bf16[256,384]{1,0:T(8,128)(2,1)S(1)}, bf16[256,384]{1,0:T(8,128)(2,1)S(1)}, u32[]{:S(2)}, u32[]{:S(2)}) collective-permute-start(bf16[256,384]{1,0:T(8,128)(2,1)S(1)} %pad_maximum_fusion.2), channel_id=1, source_target_pairs={{0,1},{1,0},{2,3},{3,2},{4,5},{5,4},{6,7},{7,6},{8,9},{9,8},{10,11... | collective-permute-start | bytes 589832 | tf_op jit(solution)/shard_map/ppermute | solution.py:28
  51.2 0.0 collective-permute-done.5
  51.2 2.2 %collective-permute-start = (bf16[256,384]{1,0:T(8,128)(2,1)S(1)}, bf16[256,384]{1,0:T(8,128)(2,1)S(1)}, u32[]{:S(2)}, u32[]{:S(2)}) collective-permute-start(bf16[256,384]{1,0:T(8,128)(2,1)S(1)} %pad_maximum_fusion.2), channel_id=1, source_target_pairs={{0,4},{1,5},{2,6},{3,7},{4,0},{5,1},{6,2},{7,3},{8,12},{9,13},{10,... | collective-permute-start | bytes 589832 | tf_op jit(solution)/shard_map/ppermute | solution.py:28
  53.4 1.2 %collective-permute-done.4 = bf16[256,384]{1,0:T(8,128)(2,1)S(1)} collective-permute-done((bf16[256,384]{1,0:T(8,128)(2,1)S(1)}, bf16[256,384]{1,0:T(8,128)(2,1)S(1)}, u32[]{:S(2)}, u32[]{:S(2)}) %collective-permute-start.4) | collective-permute-done | bytes 196640 | tf_op jit(solution)/shard_map/ppermute | solution.py:28
  54.7 6.0 %collective-permute-start.9 = (bf16[2,256,384]{2,1,0:T(8,128)(2,1)S(1)}, bf16[2,256,384]{2,1,0:T(8,128)(2,1)S(1)}, u32[]{:S(2)}, u32[]{:S(2)}) collective-permute-start(bf16[2,256,384]{2,1,0:T(8,128)(2,1)S(1)} %pad_maximum_fusion.1), channel_id=1, source_target_pairs={{0,2},{1,3},{2,0},{3,1},{4,6},{5,7},{6,4},{7,5},{8,10},{9,11},{10,... | collective-permute-start | bytes 1179656 | tf_op jit(solution)/shard_map/ppermute | solution.py:28
  60.7 0.0 collective-permute-done.3
  60.8 1.9 %collective-permute-start.8 = (bf16[2,256,384]{2,1,0:T(8,128)(2,1)S(1)}, bf16[2,256,384]{2,1,0:T(8,128)(2,1)S(1)}, u32[]{:S(2)}, u32[]{:S(2)}) collective-permute-start(bf16[2,256,384]{2,1,0:T(8,128)(2,1)S(1)} %pad_maximum_fusion.1), channel_id=1, source_target_pairs={{0,3},{1,2},{2,1},{3,0},{4,7},{5,6},{6,5},{7,4},{8,11},{9,10},{10,... | collective-permute-start | bytes 1179656 | tf_op jit(solution)/shard_map/ppermute | solution.py:28
  62.7 0.0 collective-permute-done.2
  62.7 1.9 %collective-permute-start.7 = (bf16[2,256,384]{2,1,0:T(8,128)(2,1)S(1)}, bf16[2,256,384]{2,1,0:T(8,128)(2,1)S(1)}, u32[]{:S(2)}, u32[]{:S(2)}) collective-permute-start(bf16[2,256,384]{2,1,0:T(8,128)(2,1)S(1)} %pad_maximum_fusion.1), channel_id=1, source_target_pairs={{0,1},{1,0},{2,3},{3,2},{4,5},{5,4},{6,7},{7,6},{8,9},{9,8},{10,11... | collective-permute-start | bytes 1179656 | tf_op jit(solution)/shard_map/ppermute | solution.py:28
  64.6 0.0 collective-permute-done.1
  64.6 0.1 pad_maximum_fusion
  64.7 1.9 %collective-permute-start.6 = (bf16[3,256,384]{2,1,0:T(8,128)(2,1)S(1)}, bf16[3,256,384]{2,1,0:T(8,128)(2,1)S(1)}, u32[]{:S(2)}, u32[]{:S(2)}) collective-permute-start(bf16[3,256,384]{2,1,0:T(8,128)(2,1)S(1)} %pad_maximum_fusion), channel_id=1, source_target_pairs={{0,4},{1,5},{2,6},{3,7},{4,0},{5,1},{6,2},{7,3},{8,12},{9,13},{10,... | collective-permute-start | bytes 1769480 | tf_op jit(solution)/shard_map/ppermute | solution.py:28
  66.8 13.1 %collective-permute-done.6 = bf16[3,256,384]{2,1,0:T(8,128)(2,1)S(1)} collective-permute-done((bf16[3,256,384]{2,1,0:T(8,128)(2,1)S(1)}, bf16[3,256,384]{2,1,0:T(8,128)(2,1)S(1)}, u32[]{:S(2)}, u32[]{:S(2)}) %collective-permute-start.6) | collective-permute-done | bytes 589856 | tf_op jit(solution)/shard_map/ppermute | solution.py:28
  80.0 0.1 constant_dynamic-update-slice_fusion.8
  80.0 0.1 constant_dynamic-update-slice_fusion.7
  80.1 0.0 copy-start
  80.1 0.1 constant_dynamic-update-slice_fusion.6
  80.2 0.0 collective-permute-done.9
  80.2 0.1 constant_dynamic-update-slice_fusion.5.refs_1_
  80.3 4.4 %collective-permute-start.11 = (bf16[9,256,384]{2,1,0:T(8,128)(2,1)S(1)}, bf16[9,256,384]{2,1,0:T(8,128)(2,1)S(1)}, u32[]{:S(2)}, u32[]{:S(2)}) collective-permute-start(bf16[9,256,384]{2,1,0:T(8,128)(2,1)S(1)} %constant_dynamic-update-slice_fusion.5.refs_1_), channel_id=1, source_target_pairs={{0,16},{16,0},{32,48},{48,32},{64,80},{80,64},{96,112},{112,96},{1... | collective-permute-start | bytes 5308424 | tf_op jit(solution)/shard_map/ppermute | solution.py:28
  84.8 1.9 %collective-permute-start.10 = (bf16[7,256,384]{2,1,0:T(8,128)(2,1)S(1)}, bf16[7,256,384]{2,1,0:T(8,128)(2,1)S(1)}, u32[]{:S(2)}, u32[]{:S(2)}) collective-permute-start(bf16[7,256,384]{2,1,0:T(8,128)(2,1)S(1)} %constant_dynamic-update-slice_fusion.refs_0_), channel_id=1, source_target_pairs={{0,16},{16,0},{32,48},{48,32},{64,80},{80,64},{96,112},{112,96},{1... | collective-permute-start | bytes 4128776 | tf_op jit(solution)/shard_map/ppermute | solution.py:28
  86.7 3.3 %collective-permute-done.10.refs_2_ = bf16[7,256,384]{2,1,0:T(8,128)(2,1)S(1)} collective-permute-done((bf16[7,256,384]{2,1,0:T(8,128)(2,1)S(1)}, bf16[7,256,384]{2,1,0:T(8,128)(2,1)S(1)}, u32[]{:S(2)}, u32[]{:S(2)}) %collective-permute-start.10) | collective-permute-done | bytes 1376288 | tf_op jit(solution)/shard_map/ppermute | solution.py:28
  90.0 0.0 collective-permute-done.11.refs_3_
  90.0 9.5 %merge.1 = bf16[2,2,2048,128]{3,2,1,0:T(8,128)(2,1)} custom-call(s32[32,16]{1,0:T(8,128)S(1)} %bitcast.31, bf16[2,2048,128]{2,1,0:T(8,128)(2,1)S(1)} %bitcast.30, bf16[7,256,384]{2,1,0:T(8,128)(2,1)S(1)} %constant_dynamic-update-slice_fusion.refs_0_, bf16[9,256,384]{2,1,0:T(8,128)(2,1)S(1)} %constant_dynamic-update-slice_fusion.5.refs_1_, ...), custom_call_target="tpu_custom_call" | custom-call | tf_op jit(solution)/shard_map/merge/pallas_call | solution.py:153
  (16 shorter events, 0.3 us)
Async XLA Ops:
  0.0 10.5 %copy-start.1 = (s32[32,1,16]{0,2,1:T(8,128)S(1)}, s32[32,1,16]{0,2,1:T(8,128)}, u32[]{:S(2)}) copy-start(s32[32,1,16]{0,2,1:T(8,128)} %param.3) | copy-start | bytes 6148
  0.0 32.9 %all-to-all-start = ((bf16[16,256,128]{2,1,0:T(8,128)(2,1)}), bf16[16,256,128]{2,1,0:T(8,128)(2,1)S(1)}, u32[]{:S(2)}, u32[]{:S(2)}) async-start(bf16[16,256,128]{2,1,0:T(8,128)(2,1)} %bitcast.29), calls=%async_computation | async-start | bytes 2097152 | tf_op jit(solution)/shard_map/all_to_all | solution.py:131
  32.9 18.3 %collective-permute-start.5 = (bf16[256,384]{1,0:T(8,128)(2,1)S(1)}, bf16[256,384]{1,0:T(8,128)(2,1)S(1)}, u32[]{:S(2)}, u32[]{:S(2)}) collective-permute-start(bf16[256,384]{1,0:T(8,128)(2,1)S(1)} %pad_maximum_fusion.2), channel_id=1, source_target_pairs={{0,12},{1,13},{2,14},{3,15},{4,8},{5,9},{6,10},{7,11},{8,4},{9,5},... | collective-permute-start | bytes 589832 | tf_op jit(solution)/shard_map/ppermute | solution.py:28
  38.1 16.6 %collective-permute-start.4 = (bf16[256,384]{1,0:T(8,128)(2,1)S(1)}, bf16[256,384]{1,0:T(8,128)(2,1)S(1)}, u32[]{:S(2)}, u32[]{:S(2)}) collective-permute-start(bf16[256,384]{1,0:T(8,128)(2,1)S(1)} %pad_maximum_fusion.2), channel_id=1, source_target_pairs={{0,8},{1,9},{2,10},{3,11},{4,12},{5,13},{6,14},{7,15},{8,0},{9,1},... | collective-permute-start | bytes 589832 | tf_op jit(solution)/shard_map/ppermute | solution.py:28
  42.2 18.6 %collective-permute-start.3 = (bf16[256,384]{1,0:T(8,128)(2,1)S(1)}, bf16[256,384]{1,0:T(8,128)(2,1)S(1)}, u32[]{:S(2)}, u32[]{:S(2)}) collective-permute-start(bf16[256,384]{1,0:T(8,128)(2,1)S(1)} %pad_maximum_fusion.2), channel_id=1, source_target_pairs={{0,3},{1,2},{2,1},{3,0},{4,7},{5,6},{6,5},{7,4},{8,11},{9,10},{10,... | collective-permute-start | bytes 589832 | tf_op jit(solution)/shard_map/ppermute | solution.py:28
  45.4 17.3 %collective-permute-start.2 = (bf16[256,384]{1,0:T(8,128)(2,1)S(1)}, bf16[256,384]{1,0:T(8,128)(2,1)S(1)}, u32[]{:S(2)}, u32[]{:S(2)}) collective-permute-start(bf16[256,384]{1,0:T(8,128)(2,1)S(1)} %pad_maximum_fusion.2), channel_id=1, source_target_pairs={{0,2},{1,3},{2,0},{3,1},{4,6},{5,7},{6,4},{7,5},{8,10},{9,11},{10,... | collective-permute-start | bytes 589832 | tf_op jit(solution)/shard_map/ppermute | solution.py:28
  48.2 16.4 %collective-permute-start.1 = (bf16[256,384]{1,0:T(8,128)(2,1)S(1)}, bf16[256,384]{1,0:T(8,128)(2,1)S(1)}, u32[]{:S(2)}, u32[]{:S(2)}) collective-permute-start(bf16[256,384]{1,0:T(8,128)(2,1)S(1)} %pad_maximum_fusion.2), channel_id=1, source_target_pairs={{0,1},{1,0},{2,3},{3,2},{4,5},{5,4},{6,7},{7,6},{8,9},{9,8},{10,11... | collective-permute-start | bytes 589832 | tf_op jit(solution)/shard_map/ppermute | solution.py:28
  51.2 15.4 %collective-permute-start = (bf16[256,384]{1,0:T(8,128)(2,1)S(1)}, bf16[256,384]{1,0:T(8,128)(2,1)S(1)}, u32[]{:S(2)}, u32[]{:S(2)}) collective-permute-start(bf16[256,384]{1,0:T(8,128)(2,1)S(1)} %pad_maximum_fusion.2), channel_id=1, source_target_pairs={{0,4},{1,5},{2,6},{3,7},{4,0},{5,1},{6,2},{7,3},{8,12},{9,13},{10,... | collective-permute-start | bytes 589832 | tf_op jit(solution)/shard_map/ppermute | solution.py:28
  54.7 25.5 %collective-permute-start.9 = (bf16[2,256,384]{2,1,0:T(8,128)(2,1)S(1)}, bf16[2,256,384]{2,1,0:T(8,128)(2,1)S(1)}, u32[]{:S(2)}, u32[]{:S(2)}) collective-permute-start(bf16[2,256,384]{2,1,0:T(8,128)(2,1)S(1)} %pad_maximum_fusion.1), channel_id=1, source_target_pairs={{0,2},{1,3},{2,0},{3,1},{4,6},{5,7},{6,4},{7,5},{8,10},{9,11},{10,... | collective-permute-start | bytes 1179656 | tf_op jit(solution)/shard_map/ppermute | solution.py:28
  60.8 19.4 %collective-permute-start.8 = (bf16[2,256,384]{2,1,0:T(8,128)(2,1)S(1)}, bf16[2,256,384]{2,1,0:T(8,128)(2,1)S(1)}, u32[]{:S(2)}, u32[]{:S(2)}) collective-permute-start(bf16[2,256,384]{2,1,0:T(8,128)(2,1)S(1)} %pad_maximum_fusion.1), channel_id=1, source_target_pairs={{0,3},{1,2},{2,1},{3,0},{4,7},{5,6},{6,5},{7,4},{8,11},{9,10},{10,... | collective-permute-start | bytes 1179656 | tf_op jit(solution)/shard_map/ppermute | solution.py:28
  62.7 17.3 %collective-permute-start.7 = (bf16[2,256,384]{2,1,0:T(8,128)(2,1)S(1)}, bf16[2,256,384]{2,1,0:T(8,128)(2,1)S(1)}, u32[]{:S(2)}, u32[]{:S(2)}) collective-permute-start(bf16[2,256,384]{2,1,0:T(8,128)(2,1)S(1)} %pad_maximum_fusion.1), channel_id=1, source_target_pairs={{0,1},{1,0},{2,3},{3,2},{4,5},{5,4},{6,7},{7,6},{8,9},{9,8},{10,11... | collective-permute-start | bytes 1179656 | tf_op jit(solution)/shard_map/ppermute | solution.py:28
  64.7 15.3 %collective-permute-start.6 = (bf16[3,256,384]{2,1,0:T(8,128)(2,1)S(1)}, bf16[3,256,384]{2,1,0:T(8,128)(2,1)S(1)}, u32[]{:S(2)}, u32[]{:S(2)}) collective-permute-start(bf16[3,256,384]{2,1,0:T(8,128)(2,1)S(1)} %pad_maximum_fusion), channel_id=1, source_target_pairs={{0,4},{1,5},{2,6},{3,7},{4,0},{5,1},{6,2},{7,3},{8,12},{9,13},{10,... | collective-permute-start | bytes 1769480 | tf_op jit(solution)/shard_map/ppermute | solution.py:28
  80.1 9.9 %copy-start = (bf16[2,1,1,2048,128]{4,3,2,1,0:T(8,128)(2,1)S(1)}, bf16[2,1,1,2048,128]{4,3,2,1,0:T(8,128)(2,1)}, u32[]{:S(2)}) copy-start(bf16[2,1,1,2048,128]{4,3,2,1,0:T(8,128)(2,1)} %param.2) | copy-start | bytes 3145732
  80.3 9.7 %collective-permute-start.11 = (bf16[9,256,384]{2,1,0:T(8,128)(2,1)S(1)}, bf16[9,256,384]{2,1,0:T(8,128)(2,1)S(1)}, u32[]{:S(2)}, u32[]{:S(2)}) collective-permute-start(bf16[9,256,384]{2,1,0:T(8,128)(2,1)S(1)} %constant_dynamic-update-slice_fusion.5.refs_1_), channel_id=1, source_target_pairs={{0,16},{16,0},{32,48},{48,32},{64,80},{80,64},{96,112},{112,96},{1... | collective-permute-start | bytes 5308424 | tf_op jit(solution)/shard_map/ppermute | solution.py:28
  84.8 5.2 %collective-permute-start.10 = (bf16[7,256,384]{2,1,0:T(8,128)(2,1)S(1)}, bf16[7,256,384]{2,1,0:T(8,128)(2,1)S(1)}, u32[]{:S(2)}, u32[]{:S(2)}) collective-permute-start(bf16[7,256,384]{2,1,0:T(8,128)(2,1)S(1)} %constant_dynamic-update-slice_fusion.refs_0_), channel_id=1, source_target_pairs={{0,16},{16,0},{32,48},{48,32},{64,80},{80,64},{96,112},{112,96},{1... | collective-permute-start | bytes 4128776 | tf_op jit(solution)/shard_map/ppermute | solution.py:28
